TPU v7x, 32 devices: a whole 2x2x4 slice. The times are simulated.
32 devices in a mesh: gx: 4 (over y, x), gy: 2 (over core), gz: 4 (over z).
Axes of the slice: x: 2, y: 2, z: 4, core: 2. Of those that a mesh axis runs over, the one named last changes fastest.
Arguments:
- patches: bfloat16 [512, 6144], P(('gz', 'gx'), 'gy'), may hold values from -6 to 6
- modality: int32 [512], P(('gz', 'gx')), may hold values from 0 to 2
- gains: float32 [3, 6144], P(None, 'gy'), may hold values from 0.1 to 1.9
- biases: float32 [3, 6144], P(None, 'gy'), may hold values from -3 to 3
- weights: bfloat16 [3, 6144, 3072], P(None, ('gy', 'gz'), 'gx'), may hold values from -0.078125 to 0.078125
- segments: int32 [4, 128], P('gz'), may hold values from 0 to 3, never falling along the last dimension, each value on 1 to 64 neighbouring positions
- cotangent: bfloat16 [512, 3072], P(('gz', 'gy'), 'gx'), may hold values from -6 to 6
Outputs:
- attended: bfloat16 [512, 3072], P(('gz', 'gy'), 'gx')
- patch_gradient: float32 [512, 6144], P(('gz', 'gx'), 'gy')
Inputs may be any that keep to these rules, and one draw needn't show every extreme that they name: `segments`: within each pack the segment ids never fall, and each segment holds at most half of 128 patches.
All inputs are finite; a program needn't handle non-finite values.
Results may differ from a plain program's by a relative error of at most 0.02.
Values may be sent and summed in bfloat16 or wider, within the bound.
A program may use at most 64 MiB of HBM per device.

v0:
```python
import jax
import jax.numpy as jnp
from jax import lax
from jax.sharding import PartitionSpec as P

MODEL_WIDTH = 6144
HEAD_DIM = 128
EPS = 1e-06


def sum_over_width(totals):
    return lax.psum((totals[0], totals[1]), "gy")


def split_sum(partial_value):
    return lax.psum(partial_value, "gy").astype(jnp.float32)


def on_device(patches, modality, gains, biases, weights, segments, cotangent):
    values_f = patches.astype(jnp.float32)
    totals, squares = sum_over_width((jnp.sum(values_f, -1), jnp.sum(values_f * values_f, -1)))
    average = totals / MODEL_WIDTH
    variance = squares / MODEL_WIDTH - average * average
    mean_removed = values_f - average[:, None]
    inverse_deviation = lax.rsqrt(variance + EPS)[:, None]
    standardized_input = mean_removed * inverse_deviation
    levels = jnp.arange(gains.shape[0], dtype=jnp.int32)
    chosen = (modality[:, None] == levels[None, :])[:, :, None]
    gain_per_row = jnp.sum(jnp.where(chosen, gains[None], 0.0), 1)
    bias_per_row = jnp.sum(jnp.where(chosen, biases[None], 0.0), 1)
    layer_normalized = (standardized_input * gain_per_row + bias_per_row).astype(jnp.bfloat16)
    full_weights = lax.all_gather(weights, "gz", axis=1, tiled=True)
    partial_value = jnp.einsum(
        "rd,kdc->rkc",
        lax.all_gather(layer_normalized, "gx", axis=0, tiled=True),
        full_weights,
        preferred_element_type=jnp.float32,
    ).astype(jnp.bfloat16)
    pack_rows = partial_value.shape[0]
    own_rows = pack_rows // lax.axis_size("gy")
    offset = lax.axis_index("gy") * own_rows
    projected = split_sum(partial_value).astype(jnp.bfloat16)
    queries = lax.dynamic_slice_in_dim(projected[:, 0], offset, own_rows, 0)
    keys, values = (projected[:, 1], projected[:, 2])
    columns = full_weights.shape[2]
    head_count = columns // HEAD_DIM
    queries = queries.reshape(own_rows, head_count, HEAD_DIM)
    keys = keys.reshape(pack_rows, head_count, HEAD_DIM)
    values = values.reshape(pack_rows, head_count, HEAD_DIM)
    segment = segments[0]
    segment_query = lax.dynamic_slice_in_dim(segment, offset, own_rows, 0)
    allowed = (segment_query[:, None] == segment[None, :])[None]
    scaling = HEAD_DIM ** (-0.5)
    scores = jnp.einsum("qhd,khd->hqk", queries, keys, preferred_element_type=jnp.float32) * scaling
    exponent = jnp.where(allowed, jnp.exp(scores), 0.0)
    probs = exponent / jnp.sum(exponent, -1, keepdims=True)
    probs_b = probs.astype(jnp.bfloat16)
    attended = (
        jnp.einsum("hqk,khd->qhd", probs_b, values, preferred_element_type=jnp.float32)
        .astype(jnp.bfloat16)
        .reshape(own_rows, columns)
    )
    upstream = cotangent.reshape(own_rows, head_count, HEAD_DIM)
    dprobs = jnp.einsum("qhd,khd->hqk", upstream, values, preferred_element_type=jnp.float32)
    dvalues = jnp.einsum("hqk,qhd->khd", probs_b, upstream, preferred_element_type=jnp.float32)
    dscores = (probs * (dprobs - jnp.sum(probs * dprobs, -1, keepdims=True)) * scaling).astype(
        jnp.bfloat16
    )
    dqueries = jnp.einsum("hqk,khd->qhd", dscores, keys, preferred_element_type=jnp.float32)
    dkeys = jnp.einsum("hqk,qhd->khd", dscores, queries, preferred_element_type=jnp.float32)
    query_block = lax.dynamic_update_slice_in_dim(
        jnp.zeros((pack_rows, head_count, HEAD_DIM), jnp.float32), dqueries, offset, 0
    )
    stacked = (
        jnp.stack([query_block, dkeys, dvalues], 1)
        .reshape(pack_rows, 3, columns)
        .astype(jnp.bfloat16)
    )
    grad_proj = split_sum(stacked).astype(jnp.bfloat16)
    dnormed = lax.psum_scatter(
        jnp.einsum("rkc,kdc->rd", grad_proj, full_weights, preferred_element_type=jnp.float32),
        "gx",
        scatter_dimension=0,
        tiled=True,
    )
    normalized_gradient = dnormed * gain_per_row
    gradient_row_sum, weighted_row_sum = sum_over_width(
        (jnp.sum(normalized_gradient, -1), jnp.sum(normalized_gradient * standardized_input, -1))
    )
    patch_gradient = inverse_deviation * (
        normalized_gradient
        - gradient_row_sum[:, None] / MODEL_WIDTH
        - standardized_input * (weighted_row_sum[:, None] / MODEL_WIDTH)
    )
    return (attended, patch_gradient)


def solution(mesh):
    return jax.shard_map(
        on_device,
        mesh=mesh,
        in_specs=(
            P(("gz", "gx"), "gy"),
            P(("gz", "gx")),
            P(None, "gy"),
            P(None, "gy"),
            P(None, ("gy", "gz"), "gx"),
            P("gz", None),
            P(("gz", "gy"), "gx"),
        ),
        out_specs=(P(("gz", "gy"), "gx"), P(("gz", "gx"), "gy")),
        check_vma=False,
    )
```

profile of v0, /device:TPU:0, one launch (start us, length us, event | category | flops | bytes accessed | tf_op | source)
XLA Modules:
  0.0 362.8 jit_solution(14495759897900691260)
XLA Ops:
  7.2 0.0 copy-start
  7.2 0.0 copy-start.1
  7.2 0.0 copy-start.5
  7.2 0.0 copy-start.3
  7.2 0.0 copy-start.2
  7.2 0.0 all-gather.2.cloned.1.call-start
  7.3 0.7 all-gather.2.cloned.1.call-update
  8.0 0.0 all-reduce.5.cloned.1.call-start
  8.0 0.1 copy-done.1
  8.1 0.2 convert_reduce_fusion
  8.3 2.6 all-reduce.1
  10.9 0.0 copy-done.3
  11.0 0.2 select_reduce_fusion.1
  11.2 0.1 fusion.14
  11.4 13.4 %all_gather.6 = bf16[128,3072]{1,0:T(8,128)(2,1)S(1)} all-gather(bf16[32,3072]{1,0:T(8,128)(2,1)S(1)} %fusion.14), channel_id=1, replica_groups=mesh['gx'=4,'gy'=2,'gz'=4] {'gx'}, dimensions={0}, use_global_device_ids=true | all-gather | bytes 983040 | tf_op jit(solution)/shard_map/all_gather | solution.py:35
  24.7 231.5 %all-gather.2.cloned.1.call-done = bf16[3,3072,768]{2,1,0:T(8,128)(2,1)} async-done(((bf16[3,768,768]{2,1,0:T(8,128)(2,1)}), bf16[3,3072,768]{2,1,0:T(8,128)(2,1)}) %all-gather.2.cloned.1.call-update) | async-done | bytes 14155792 | tf_op jit(solution)/shard_map/all_gather | solution.py:32
  256.3 7.9 %convolution_convert_fusion = bf16[128,3,768]{2,0,1:T(8,128)(2,1)} fusion(bf16[3,3072,768]{2,1,0:T(8,128)(2,1)} %all-gather.2.cloned.1.call-done, bf16[128,3072]{1,0:T(8,128)(2,1)S(1)} %all_gather.6), kind=kOutput, calls=%fused_computation.2 | convolution fusion | flops 1812234240 | bytes 15532032 | tf_op jit(solution)/shard_map/rd,kdc->rkc/dot_general | solution.py:33
  264.1 0.0 all-reduce.5.cloned.1.call-update
  264.1 0.0 all-reduce.7.cloned.1.call-start
  264.2 0.1 dynamic-slice_bitcast_fusion
  264.3 0.1 broadcast_compare_fusion
  264.4 16.8 %all-reduce.5.cloned.1.call-done = bf16[128,3,768]{2,0,1:T(8,128)(2,1)} async-done(((bf16[128,3,768]{2,0,1:T(8,128)(2,1)}), bf16[128,3,768]{2,0,1:T(8,128)(2,1)}) %all-reduce.5.cloned.1.call-update) | async-done | bytes 589840 | tf_op jit(solution)/shard_map/psum | solution.py:16
  281.2 1.2 fusion.40
  282.4 0.1 reshape.89
  282.5 0.2 copy.34
  282.7 0.2 copy.33
  282.8 0.3 fusion.26
  283.1 0.3 convolution_convert_fusion.1
  283.4 0.2 convolution_bitcast_fusion.1
  283.6 0.3 convolution_bitcast_fusion.2
  283.9 0.3 convolution_convert_fusion.2
  284.2 0.1 copy.47
  284.4 0.1 copy.46
  284.5 0.2 copy.42
  284.7 1.3 dynamic_update_slice.4
  286.1 0.1 copy.45
  286.2 0.9 pad_maximum_fusion
  287.1 0.0 all-reduce.7.cloned.1.call-update
  287.1 0.0 reduce-scatter.2.cloned.1.call-start
  287.2 21.1 %all-reduce.7.cloned.1.call-done = bf16[128,3,768]{2,0,1:T(8,128)(2,1)} async-done(((bf16[128,3,768]{2,0,1:T(8,128)(2,1)}), bf16[128,3,768]{2,0,1:T(8,128)(2,1)}) %all-reduce.7.cloned.1.call-update) | async-done | bytes 589840 | tf_op jit(solution)/shard_map/psum | solution.py:16
  308.2 10.9 %convolution_bitcast_fusion = f32[128,3072]{1,0:T(8,128)} fusion(bf16[128,3,768]{2,0,1:T(8,128)(2,1)} %all-reduce.7.cloned.1.call-done, bf16[3,3072,768]{2,1,0:T(8,128)(2,1)} %all-gather.2.cloned.1.call-done), kind=kOutput, calls=%fused_computation.1 | convolution fusion | flops 1811939328 | bytes 16318464 | tf_op jit(solution)/shard_map/rkc,kdc->rd/dot_general | solution.py:81
  319.2 0.0 reduce-scatter.2.cloned.1.call-update
  319.2 0.2 fusion.7
  319.4 0.7 copy.69
  320.1 31.6 %reduce-scatter.2.cloned.1.call-done = f32[32,3072]{1,0:T(8,128)} async-done(((f32[128,3072]{1,0:T(8,128)}), f32[32,3072]{1,0:T(8,128)}) %reduce-scatter.2.cloned.1.call-update) | async-done | bytes 393232 | tf_op jit(solution)/shard_map/reduce_scatter | solution.py:80
  351.7 1.2 fusion.39
  352.9 2.5 all-reduce
  355.4 0.9 fusion.17
  (10 shorter events, 0.1 us)
Async XLA Ops:
  7.2 276.0 %copy-start = (bf16[64,768]{1,0:T(8,128)(2,1)S(1)}, bf16[64,768]{1,0:T(8,128)(2,1)}, u32[]{:S(2)}) copy-start(bf16[64,768]{1,0:T(8,128)(2,1)} %param.13) | copy-start | bytes 294916
  7.2 1.0 copy-start.1
  7.2 3.7 %copy-start.5 = (s32[32]{0:T(128)S(1)}, s32[32]{0:T(128)}, u32[]{:S(2)}) copy-start(s32[32]{0:T(128)} %param.8) | copy-start | bytes 388
  7.2 3.7 %copy-start.3 = (f32[3,3072]{1,0:T(4,128)S(1)}, f32[3,3072]{1,0:T(4,128)}, u32[]{:S(2)}) copy-start(f32[3,3072]{1,0:T(4,128)} %param.10) | copy-start | bytes 110596
  7.2 3.7 %copy-start.2 = (f32[3,3072]{1,0:T(4,128)S(1)}, f32[3,3072]{1,0:T(4,128)}, u32[]{:S(2)}) copy-start(f32[3,3072]{1,0:T(4,128)} %param.9) | copy-start | bytes 110596
  7.2 249.0 %all-gather.2.cloned.1.call-start = ((), (), s32[]{:S(2)}) async-start(), calls=%async_computation.1 | async-start | bytes 17694720 | tf_op jit(solution)/shard_map/all_gather | solution.py:32
  8.0 273.2 %all-reduce.5.cloned.1.call-start = ((), (), s32[]{:S(2)}) async-start(), calls=%async_computation.2 | async-start | bytes 1179648 | tf_op jit(solution)/shard_map/psum | solution.py:16
  24.7 239.4 %copy-start.4 = (s32[1,128]{1,0:T(1,128)S(1)}, s32[1,128]{1,0:T(1,128)}, u32[]{:S(2)}) copy-start(s32[1,128]{1,0:T(1,128)} %param.12) | copy-start | bytes 1540
  264.1 44.1 %all-reduce.7.cloned.1.call-start = ((), (), s32[]{:S(2)}) async-start(), calls=%async_computation.3 | async-start | bytes 1179648 | tf_op jit(solution)/shard_map/psum | solution.py:16
  287.1 64.6 %reduce-scatter.2.cloned.1.call-start = ((), (), s32[]{:S(2)}) async-start(), calls=%async_computation.4 | async-start | bytes 1966080 | tf_op jit(solution)/shard_map/reduce_scatter | solution.py:80
Sparse Core Ops, SparseCore 0:
  9.6 246.6 all-gather.1
  264.3 16.8 all-reduce.4
  287.2 20.9 all-reduce.6
  319.3 32.3 reduce-scatter.1
where the time goes:
time: 363 us
  waiting for transfers between devices  302 us (83%)
  matrix products  20.3 us (6%)
  blocking collectives  18.5 us (5%)
  between operations  14 us (4%)
  local copies, waits for them, and re-layouts  4.51 us (1%)
  other arithmetic  3.66 us (1%)
    all_gather x1, waiting for transfers between devices, on_device(): full_weights = lax.all_gather(weights, 'gz', axis=1, tiled=True)  232 us
    psum x2, waiting for transfers between devices, split_sum(): return lax.psum(partial_value, 'gy').astype(jnp.float32)  37.9 us
    reduce_scatter x1, waiting for transfers between devices, on_device(): lax.psum_scatter(jnp.einsum('rkc,kdc->rd', grad_proj, full_weights, prefe...  31.6 us
    all_gather x1, blocking collectives, on_device(): lax.all_gather(layer_normalized, 'gx', axis=0, tiled=True)  13.4 us
    dot_general x1, matrix products, on_device(): jnp.einsum('rkc,kdc->rd', grad_proj, full_weights, preferred_element_type...  10.9 us
    dot_general x1, matrix products, on_device(): jnp.einsum('rd,kdc->rkc', lax.all_gather(layer_normalized, 'gx', axis=0,...  7.86 us
  transfers between devices with their start and end apart: 4, of which 4 were waited for; matrix products, arithmetic and copies ran while one was open for 0% of the time, Pallas kernels for 0%

commit v1 on v0

--- a/solution.py
+++ b/solution.py
@@ -13,7 +13,7 @@
 
 
 def split_sum(partial_value):
-    return lax.psum(partial_value, "gy").astype(jnp.float32)
+    return jnp.sum(lax.all_gather(partial_value, "gy"), axis=0).astype(jnp.float32)
 
 
 def on_device(patches, modality, gains, biases, weights, segments, cotangent):

time: 363 us -> 346 us (0.953)
  waiting for transfers between devices: 302 us -> 283 us
    psum x2 -> x0, waiting for transfers between devices: 37.9 us -> none  [split_sum(): return lax.psum(partial_value, 'gy').astype(jnp.float32)]
    all_gather x0 -> x2, waiting for transfers between devices: none -> 19 us  [split_sum(): lax.all_gather(partial_value, 'gy')]
where the time goes in v1:
time: 346 us; the launch traced here: 345 us
  waiting for transfers between devices  283 us (82%)
  matrix products  20.1 us (6%)
  blocking collectives  18.5 us (5%)
  between operations  14 us (4%)
  other arithmetic  5.88 us (2%)
  local copies, waits for them, and re-layouts  4.03 us (1%)
    all_gather x1, waiting for transfers between devices, on_device(): full_weights = lax.all_gather(weights, 'gz', axis=1, tiled=True)  232 us
    reduce_scatter x1, waiting for transfers between devices, on_device(): lax.psum_scatter(jnp.einsum('rkc,kdc->rd', grad_proj, full_weights, prefe...  31.6 us
    all_gather x2, waiting for transfers between devices, split_sum(): lax.all_gather(partial_value, 'gy')  19 us
    all_gather x1, blocking collectives, on_device(): lax.all_gather(layer_normalized, 'gx', axis=0, tiled=True)  13.4 us
    dot_general x1, matrix products, on_device(): jnp.einsum('rkc,kdc->rd', grad_proj, full_weights, preferred_element_type...  10.7 us
    dot_general x1, matrix products, on_device(): jnp.einsum('rd,kdc->rkc', lax.all_gather(layer_normalized, 'gx', axis=0,...  7.86 us
  transfers between devices with their start and end apart: 4, of which 4 were waited for; matrix products, arithmetic and copies ran while one was open for 0% of the time, Pallas kernels for 0%

profile of v1, /device:TPU:0, one launch (start us, length us, event | category | flops | bytes accessed | tf_op | source)
XLA Modules:
  0.0 345.4 jit_solution(2215020896399271148)
XLA Ops:
  7.2 0.0 copy-start
  7.2 0.0 copy-start.1
  7.2 0.0 copy-start.5
  7.2 0.0 copy-start.3
  7.2 0.0 copy-start.2
  7.2 0.0 all-gather.5.cloned.1.call-start
  7.3 0.7 all-gather.5.cloned.1.call-update
  8.0 0.0 all-gather.9.cloned.1.call-start
  8.0 0.1 copy-done.1
  8.1 0.2 convert_reduce_fusion
  8.3 2.6 all-reduce.1
  10.9 0.0 copy-done.5
  10.9 0.0 copy-done.3
  11.0 0.2 select_reduce_fusion.1
  11.2 0.1 fusion.14
  11.4 13.4 %all_gather.16 = bf16[128,3072]{1,0:T(8,128)(2,1)S(1)} all-gather(bf16[32,3072]{1,0:T(8,128)(2,1)S(1)} %fusion.14), channel_id=1, replica_groups=mesh['gx'=4,'gy'=2,'gz'=4] {'gx'}, dimensions={0}, use_global_device_ids=true | all-gather | bytes 983040 | tf_op jit(solution)/shard_map/all_gather | solution.py:35
  24.7 231.5 %all-gather.5.cloned.1.call-done = bf16[3,3072,768]{2,1,0:T(8,128)(2,1)} async-done(((bf16[3,768,768]{2,1,0:T(8,128)(2,1)}), bf16[3,3072,768]{2,1,0:T(8,128)(2,1)}) %all-gather.5.cloned.1.call-update) | async-done | bytes 14155792 | tf_op jit(solution)/shard_map/all_gather | solution.py:32
  256.3 7.9 %convolution_convert_fusion = bf16[128,3,768]{2,0,1:T(8,128)(2,1)} fusion(bf16[3,3072,768]{2,1,0:T(8,128)(2,1)} %all-gather.5.cloned.1.call-done, bf16[128,3072]{1,0:T(8,128)(2,1)S(1)} %all_gather.16), kind=kOutput, calls=%fused_computation.2 | convolution fusion | flops 1812234240 | bytes 15532032 | tf_op jit(solution)/shard_map/rd,kdc->rkc/dot_general | solution.py:33
  264.1 0.0 all-gather.9.cloned.1.call-update
  264.1 0.0 all-gather.7.cloned.1.call-start
  264.2 0.1 dynamic-slice_bitcast_fusion
  264.3 0.1 broadcast_compare_fusion
  264.4 7.3 %all-gather.9.cloned.1.call-done = bf16[256,3,768]{2,0,1:T(8,128)(2,1)} async-done(((bf16[128,3,768]{2,0,1:T(8,128)(2,1)}), bf16[256,3,768]{2,0,1:T(8,128)(2,1)}) %all-gather.9.cloned.1.call-update) | async-done | bytes 1179664 | tf_op jit(solution)/shard_map/all_gather | solution.py:16
  271.7 1.5 reduce_sum.100
  273.3 0.1 reshape.134
  273.4 0.2 copy.38
  273.6 0.2 copy.37
  273.8 0.3 fusion.26
  274.1 0.3 convolution_convert_fusion.1
  274.3 0.2 convolution_bitcast_fusion.1
  274.5 0.3 convolution_bitcast_fusion.2
  274.8 0.3 convolution_convert_fusion.2
  275.2 0.2 copy.46
  275.4 1.3 dynamic_update_slice.4
  276.7 0.1 pad_maximum_fusion
  276.8 1.1 copy.49
  277.8 0.0 all-gather.7.cloned.1.call-update
  277.9 0.0 reduce-scatter.2.cloned.1.call-start
  277.9 11.6 %all-gather.7.cloned.1.call-done = bf16[2,128,3,768]{3,1,2,0:T(8,128)(2,1)} async-done(((bf16[1,128,3,768]{3,1,2,0:T(8,128)(2,1)}), bf16[2,128,3,768]{3,1,2,0:T(8,128)(2,1)}) %all-gather.7.cloned.1.call-update) | async-done | bytes 1179664 | tf_op jit(solution)/shard_map/all_gather | solution.py:16
  289.5 1.5 reduce_sum.103
  291.0 10.7 %convolution_bitcast_fusion = f32[128,3072]{1,0:T(8,128)} fusion(bf16[128,3,768]{2,0,1:T(8,128)(2,1)S(1)} %reduce_sum.103, bf16[3,3072,768]{2,1,0:T(8,128)(2,1)} %all-gather.5.cloned.1.call-done), kind=kOutput, calls=%fused_computation.1 | convolution fusion | flops 1811939328 | bytes 16318464 | tf_op jit(solution)/shard_map/rkc,kdc->rd/dot_general | solution.py:81
  301.8 0.0 reduce-scatter.2.cloned.1.call-update
  301.8 0.2 fusion.7
  302.0 0.7 copy.75
  302.7 31.6 %reduce-scatter.2.cloned.1.call-done = f32[32,3072]{1,0:T(8,128)} async-done(((f32[128,3072]{1,0:T(8,128)}), f32[32,3072]{1,0:T(8,128)}) %reduce-scatter.2.cloned.1.call-update) | async-done | bytes 393232 | tf_op jit(solution)/shard_map/reduce_scatter | solution.py:80
  334.3 1.2 fusion.39
  335.5 2.5 all-reduce
  338.0 0.9 fusion.17
  (10 shorter events, 0.1 us)
Async XLA Ops:
  7.2 266.9 %copy-start = (bf16[64,768]{1,0:T(8,128)(2,1)S(1)}, bf16[64,768]{1,0:T(8,128)(2,1)}, u32[]{:S(2)}) copy-start(bf16[64,768]{1,0:T(8,128)(2,1)} %param.13) | copy-start | bytes 294916
  7.2 1.0 copy-start.1
  7.2 3.7 %copy-start.5 = (s32[32]{0:T(128)S(1)}, s32[32]{0:T(128)}, u32[]{:S(2)}) copy-start(s32[32]{0:T(128)} %param.8) | copy-start | bytes 388
  7.2 3.7 %copy-start.3 = (f32[3,3072]{1,0:T(4,128)S(1)}, f32[3,3072]{1,0:T(4,128)}, u32[]{:S(2)}) copy-start(f32[3,3072]{1,0:T(4,128)} %param.10) | copy-start | bytes 110596
  7.2 3.7 %copy-start.2 = (f32[3,3072]{1,0:T(4,128)S(1)}, f32[3,3072]{1,0:T(4,128)}, u32[]{:S(2)}) copy-start(f32[3,3072]{1,0:T(4,128)} %param.9) | copy-start | bytes 110596
  7.2 249.0 %all-gather.5.cloned.1.call-start = ((), (), s32[]{:S(2)}) async-start(), calls=%async_computation.1 | async-start | bytes 17694720 | tf_op jit(solution)/shard_map/all_gather | solution.py:32
  8.0 263.7 %all-gather.9.cloned.1.call-start = ((), (), s32[]{:S(2)}) async-start(), calls=%async_computation.4 | async-start | bytes 1769472 | tf_op jit(solution)/shard_map/all_gather | solution.py:16
  24.7 239.4 %copy-start.4 = (s32[1,128]{1,0:T(1,128)S(1)}, s32[1,128]{1,0:T(1,128)}, u32[]{:S(2)}) copy-start(s32[1,128]{1,0:T(1,128)} %param.12) | copy-start | bytes 1540
  264.1 25.4 %all-gather.7.cloned.1.call-start = ((), (), s32[]{:S(2)}) async-start(), calls=%async_computation.2 | async-start | bytes 1769472 | tf_op jit(solution)/shard_map/all_gather | solution.py:16
  277.9 56.4 %reduce-scatter.2.cloned.1.call-start = ((), (), s32[]{:S(2)}) async-start(), calls=%async_computation.3 | async-start | bytes 1966080 | tf_op jit(solution)/shard_map/reduce_scatter | solution.py:80
Sparse Core Ops, SparseCore 0:
  9.6 246.6 all-gather.4
  264.3 7.3 all-gather.8
  278.0 11.4 all-gather.6
  301.9 32.3 reduce-scatter.1
